TPU v7x, 32 devices: a whole 2x2x4 slice. The times are simulated.
32 devices in a mesh: groups: 2 (over y), ctx: 4 (over z), fsdp: 4 (over x, core).
Axes of the slice: x: 2, y: 2, z: 4, core: 2. Of those that a mesh axis runs over, the one named last changes fastest.
Arguments:
- patches: bfloat16 [8192, 1024], P(('groups', 'ctx', 'fsdp')), parts along dimension 0, may hold values from -6 to 6
- labels: int32 [8192], P(('groups', 'ctx', 'fsdp')), parts along dimension 0, may hold values from 0 to 127
- op_ids: int32 [4, 3], P('groups'), parts along dimension 0, may hold values from 0 to 8
- mix_codes: int32 [4, 4], P('groups'), parts along dimension 0, may hold values from 1 to 8
- aug_gains: float32 [9, 1024], replicated, may hold values from 0.1 to 1.9
- in_weight: bfloat16 [1024, 1536], P('fsdp'), may hold values from -0.1875 to 0.1875
- dt_weight: bfloat16 [1024, 32], P('fsdp'), may hold values from -0.09375 to 0.09375
- dt_bias: float32 [2, 16], replicated, may hold values from -3.9 to -2.2
- decay_log: float32 [2, 16], replicated, may hold values from -12 to 0
- skip_gain: float32 [16], replicated, may hold values from 0.1 to 1.9
- norm_gain: float32 [1024], replicated, may hold values from 0.5 to 1.5
- out_weight: bfloat16 [1024, 1024], P('fsdp'), may hold values from -0.1875 to 0.1875
- head_weight: bfloat16 [1024, 128], replicated, may hold values from -8 to 8
Outputs:
- grad_out: float32 [2048, 1024], P(('groups', 'ctx', 'fsdp')), parts along dimension 0
- grad_head: float32 [2048, 128], P(('groups', 'ctx', 'fsdp')), parts along dimension 0
- patch_loss: float32 [8192], P(('groups', 'ctx', 'fsdp')), parts along dimension 0
There are 2 independent parts, one for each index of `groups`. A program takes and returns all parts, laid end to end along the dimension named above; an argument that names none is the same for every part. Nothing has to cross between parts.
All inputs are finite; a program needn't handle non-finite values.
Results may differ from a plain program's by a relative error of at most 0.01505.
The roundings to bfloat16 on the way count: a program that leaves them out, or rounds other values in their place, can miss the bound.
Values may be sent and summed in bfloat16 or wider, within the bound.
A program may use at most 128 MiB of HBM per device.

v0:
```python
import jax
import jax.numpy as jnp
from jax import lax
from jax.sharding import PartitionSpec as P

D = 1024
HEADS = 16
HEAD_DIM = 64
STATE = 128
CLASSES = 128
VIEWS = 3
NOPS = 9
WIDTH_AUG = 3
BLOCK = 128
loss_scale = 256.0
mix_lambda = 12.0
highest = lax.Precision.HIGHEST


def carried_in_2(value, axis, combine, identity, reverse):
    count, mine = (lax.axis_size(axis), lax.axis_index(axis))
    everything = jax.tree.map(lambda part: lax.all_gather(part, axis), value)
    start = jax.tree.map(
        lambda part, zero: jnp.broadcast_to(jnp.asarray(zero, part.dtype), part.shape),
        value,
        identity,
    )

    def turn(k, before):
        at = count - 1 - k if reverse else k
        reached = at > mine if reverse else at < mine
        new = combine(before, jax.tree.map(lambda part: part[at], everything))
        return jax.tree.map(lambda a, b: jnp.where(reached, a, b), new, before)

    return lax.fori_loop(0, count, turn, start)


def view_scales(op_ids, mix_codes, aug_gains):
    code_values = mix_codes.astype(jnp.float32)
    weights = code_values[:, :WIDTH_AUG] / jnp.sum(
        code_values[:, :WIDTH_AUG], axis=1, keepdims=True
    )
    keep_share = code_values[:, WIDTH_AUG] / 9.0
    onehot = (op_ids[:, :, None] == jnp.arange(NOPS, dtype=jnp.int32)[None, None, :]).astype(
        jnp.float32
    )
    op_weights = jnp.sum(onehot * weights[:, :, None], axis=1)
    mixed_gain = jnp.dot(op_weights, aug_gains, precision=highest)
    scaled = keep_share[:, None] + (1.0 - keep_share[:, None]) * mixed_gain
    return jnp.concatenate([jnp.ones((1, D), jnp.float32), scaled], axis=0)


def block_pass(values, write_vectors, read_vectors, step_sizes, decay_rates):
    length, head_count, head_width = values.shape
    pieces = length // BLOCK
    shaped = (
        values.reshape(pieces, BLOCK, head_count, head_width),
        write_vectors.reshape(pieces, BLOCK, STATE),
        read_vectors.reshape(pieces, BLOCK, STATE),
        step_sizes.reshape(pieces, BLOCK, head_count),
    )
    lower_mask = jnp.arange(BLOCK)[:, None] >= jnp.arange(BLOCK)[None, :]

    def advance(carried_in, inputs):
        state_now, offset = carried_in
        piece_values, piece_write, piece_read, piece_steps = inputs
        value_float = piece_values.astype(jnp.float32)
        write_float = piece_write.astype(jnp.float32)
        read_float = piece_read.astype(jnp.float32)
        step_logs = piece_steps * decay_rates[None, :]
        running = jnp.cumsum(step_logs, axis=0)
        log_gaps = running[:, None, :] - running[None, :, :]
        mask_decay = jnp.exp(jnp.where(lower_mask[:, :, None], log_gaps, -1e30))
        scores = jnp.dot(read_float, write_float.T, precision=highest)
        mixing = scores[:, :, None] * mask_decay * piece_steps[None, :, :]
        inside = jnp.einsum("tsh,shp->thp", mixing, value_float, precision=highest)
        carried = jnp.exp(running)[:, :, None] * jnp.einsum(
            "tn,hpn->thp", read_float, state_now, precision=highest
        )
        last_log = running[-1]
        weighted = (jnp.exp(last_log[None, :] - running) * piece_steps)[:, :, None] * value_float
        new_state = jnp.exp(last_log)[:, None, None] * state_now + jnp.einsum(
            "shp,sn->hpn", weighted, write_float, precision=highest
        )
        return ((new_state, offset + last_log), (inside + carried, offset[None, :] + running))

    initial = (
        jnp.zeros((head_count, head_width, STATE), jnp.float32),
        jnp.zeros((head_count,), jnp.float32),
    )
    (final_state, total_log), (outputs, positions_log) = lax.scan(advance, initial, shaped)
    return (
        outputs.reshape(length, head_count, head_width),
        positions_log.reshape(length, head_count),
        final_state,
        total_log,
    )


def loss_terms(logits, labels):
    log_probs = jax.nn.log_softmax(logits, axis=-1)
    probabilities = jnp.exp(log_probs)
    log_mean = jax.scipy.special.logsumexp(log_probs, axis=0) - jnp.log(jnp.float32(VIEWS))
    spread = jnp.sum(probabilities * (log_probs - log_mean[None]), axis=(0, 2)) / VIEWS
    onehot = (labels[:, None] == jnp.arange(CLASSES, dtype=jnp.int32)[None, :]).astype(jnp.float32)
    cross_entropy = -jnp.sum(onehot * log_probs[0], axis=-1)
    return cross_entropy + mix_lambda * spread


def combine_states(earlier, later):
    earlier_log, earlier_state = earlier
    later_log, later_state = later
    return (
        earlier_log + later_log,
        jnp.exp(later_log)[:, :, None, None] * earlier_state + later_state,
    )


def apply_incoming(outputs, positions_log, read_vectors, incoming):
    reached = jnp.einsum(
        "vtn,vhpn->vthp", read_vectors.astype(jnp.float32), incoming, precision=highest
    )
    return outputs + jnp.exp(positions_log)[:, :, :, None] * reached


def on_device(
    patches,
    labels,
    op_ids,
    mix_codes,
    aug_gains,
    in_weight,
    dt_weight,
    dt_bias,
    decay_log,
    skip_gain,
    norm_gain,
    out_weight,
    head_weight,
):
    row_count = patches.shape[0]
    ctx_count = lax.axis_size("ctx")
    fsdp_count = lax.axis_size("fsdp")
    fsdp_place = lax.axis_index("fsdp")
    total_patches = row_count * ctx_count * fsdp_count
    inner_width = out_weight.shape[0] * fsdp_count
    local_heads = HEADS // fsdp_count
    range_rows = row_count * fsdp_count
    scales = view_scales(op_ids, mix_codes, aug_gains)
    views = (scales[:, None, :] * patches.astype(jnp.float32)[None]).astype(jnp.bfloat16)
    flat_rows = views.reshape(VIEWS * row_count, D)
    columns = flat_rows
    proj_sum = jnp.dot(
        columns,
        lax.all_gather(in_weight, "fsdp", axis=0, tiled=True),
        preferred_element_type=jnp.float32,
    )
    raw_sum = jnp.dot(
        columns,
        lax.all_gather(dt_weight, "fsdp", axis=0, tiled=True),
        preferred_element_type=jnp.float32,
    )
    projected = proj_sum.astype(jnp.bfloat16).reshape(VIEWS, row_count, in_weight.shape[1])
    step_sizes = jax.nn.softplus(raw_sum.reshape(VIEWS, row_count, 2, HEADS) + dt_bias[None, None])
    value_rows = projected[:, :, :inner_width].reshape(
        VIEWS, row_count, fsdp_count, local_heads * HEAD_DIM
    )
    head_rows = lax.all_to_all(value_rows, "fsdp", split_axis=2, concat_axis=1, tiled=True)
    values = head_rows.reshape(VIEWS, range_rows, local_heads, HEAD_DIM)
    step_rows = step_sizes.reshape(VIEWS, row_count, 2, fsdp_count, local_heads)
    head_step_rows = lax.all_to_all(step_rows, "fsdp", split_axis=3, concat_axis=1, tiled=True)
    local_steps = head_step_rows.reshape(VIEWS, range_rows, 2, local_heads)
    shared = lax.all_gather(projected[:, :, inner_width:], "fsdp", axis=1, tiled=True)
    coefficients = shared.reshape(VIEWS, range_rows, 4, STATE)
    head_start = fsdp_place * local_heads
    decay_rates = lax.dynamic_slice_in_dim(-jnp.exp(decay_log), head_start, local_heads, 1)
    local_skip = lax.dynamic_slice_in_dim(skip_gain, head_start, local_heads, 0)
    local_gain = lax.dynamic_slice_in_dim(
        norm_gain, head_start * HEAD_DIM, local_heads * HEAD_DIM, 0
    )
    mapped = jax.vmap(block_pass, in_axes=(0, 0, 0, 0, None))
    forward_read = coefficients[:, :, 1]
    forward_out, forward_logs, forward_state, forward_total = mapped(
        values, coefficients[:, :, 0], forward_read, local_steps[:, :, 0], decay_rates[0]
    )
    reverse_values = jnp.flip(values, 1)
    reverse_read = jnp.flip(coefficients[:, :, 3], 1)
    reverse_out, reverse_logs, reverse_state, reverse_total = mapped(
        reverse_values,
        jnp.flip(coefficients[:, :, 2], 1),
        reverse_read,
        jnp.flip(local_steps[:, :, 1], 1),
        decay_rates[1],
    )
    identity = (jnp.zeros_like(forward_total), jnp.zeros_like(forward_state))
    forward_in = carried_in_2(
        (forward_total, forward_state), "ctx", combine_states, identity, False
    )
    reverse_in = carried_in_2((reverse_total, reverse_state), "ctx", combine_states, identity, True)
    forward_full = apply_incoming(forward_out, forward_logs, forward_read, forward_in[1])
    reverse_full = apply_incoming(reverse_out, reverse_logs, reverse_read, reverse_in[1])
    mixed = (
        forward_full
        + jnp.flip(reverse_full, 1)
        + local_skip[None, None, :, None] * values.astype(jnp.float32)
    )
    mixed = mixed.reshape(VIEWS, range_rows, local_heads * HEAD_DIM)
    square_total = lax.psum(jnp.sum(mixed * mixed, axis=-1), "fsdp")
    scaling = lax.rsqrt(square_total / inner_width + 1e-05)
    normed_heads = (mixed * scaling[:, :, None] * local_gain[None, None, :]).astype(jnp.bfloat16)
    normed_rows = lax.all_to_all(normed_heads, "fsdp", split_axis=1, concat_axis=2, tiled=True)
    normed = normed_rows.reshape(VIEWS * row_count, inner_width)
    columns = normed
    out_sum = jnp.dot(
        columns,
        lax.all_gather(out_weight, "fsdp", axis=0, tiled=True),
        preferred_element_type=jnp.float32,
    )
    hidden = (flat_rows.astype(jnp.float32) + out_sum).astype(jnp.bfloat16)
    logits = jnp.dot(hidden, head_weight, preferred_element_type=jnp.float32).reshape(
        VIEWS, row_count, CLASSES
    )

    def per_patch(logit_values):
        return loss_terms(logit_values, labels)

    patch_loss, pullback = jax.vjp(per_patch, logits)
    (grad_logits,) = pullback(jnp.full((row_count,), loss_scale / total_patches, jnp.float32))
    grad_logits_bf = grad_logits.reshape(VIEWS * row_count, CLASSES).astype(jnp.bfloat16)
    grad_hidden = lax.dot_general(
        grad_logits_bf, head_weight, (((1,), (1,)), ((), ())), preferred_element_type=jnp.float32
    ).astype(jnp.bfloat16)
    head_term = lax.dot_general(
        hidden, grad_logits_bf, (((0,), (0,)), ((), ())), preferred_element_type=jnp.float32
    )
    columns = normed
    grad_out = lax.psum_scatter(
        lax.dot_general(
            columns, grad_hidden, (((0,), (0,)), ((), ())), preferred_element_type=jnp.float32
        ),
        ("ctx", "fsdp"),
        scatter_dimension=0,
        tiled=True,
    )
    grad_head = lax.psum_scatter(head_term, ("ctx", "fsdp"), scatter_dimension=0, tiled=True)
    return (grad_out, grad_head, patch_loss)


def solution(mesh):
    return jax.shard_map(
        on_device,
        mesh=mesh,
        in_specs=(
            P(("groups", "ctx", "fsdp"), None),
            P(("groups", "ctx", "fsdp")),
            P("groups", None),
            P("groups", None),
            P(),
            P("fsdp", None),
            P("fsdp", None),
            P(),
            P(),
            P(),
            P(),
            P("fsdp", None),
            P(),
        ),
        out_specs=(
            P(("groups", "ctx", "fsdp"), None),
            P(("groups", "ctx", "fsdp"), None),
            P(("groups", "ctx", "fsdp")),
        ),
        check_vma=False,
    )
```

profile of v0, /device:TPU:0, one launch (start us, length us, event | category | flops | bytes accessed | tf_op | source)
XLA Modules:
  0.0 552.4 jit_solution(7558193707011760850)
XLA Ops:
  11.7 29.2 %all-gather.12.cloned.1.call-done = bf16[1024,1536]{1,0:T(8,128)(2,1)} async-done(((bf16[256,1536]{1,0:T(8,128)(2,1)}), bf16[1024,1536]{1,0:T(8,128)(2,1)}) %all-gather.12.cloned.1.call-update) | async-done | bytes 3145744 | tf_op jit(solution)/shard_map/all_gather | solution.py:155
  40.8 4.7 convolution_convert_fusion
  48.3 5.2 all_gather.36
  54.9 3.3 all-to-all-start
  63.8 3.6 all-to-all-start.1
  68.5 24.8 %all-to-all-done.1 = bf16[3,256,4,256]{1,3,0,2:T(8,128)(2,1)S(1)} async-done(((bf16[3,256,4,256]{1,3,0,2:T(8,128)(2,1)}), bf16[3,256,4,256]{1,3,0,2:T(8,128)(2,1)S(1)}, u32[]{:S(2)}, u32[]{:S(2)}) %all-to-all-start.1) | async-done | bytes 1572896 | tf_op jit(solution)/shard_map/all_to_all | solution.py:168
  98.5 3.6 reshape_reshape.3
  102.2 3.7 rev.20
  105.9 3.1 copy.256
  110.7 3.6 fusion.116
  114.3 10.3 %rev.22 = bf16[3,1024,128]{1,2,0:T(8,128)(2,1)S(1)} reverse(bf16[3,1024,128]{1,2,0:T(8,128)(2,1)} %get-tuple-element.680), dimensions={1} | reverse | bytes 1572864 | tf_op jit(solution)/shard_map/jit(_flip)/rev | solution.py:187
  128.2 10.3 %rev.21 = bf16[3,1024,128]{1,2,0:T(8,128)(2,1)S(1)} reverse(bf16[3,1024,128]{1,2,0:T(8,128)(2,1)} %get-tuple-element.681), dimensions={1} | reverse | bytes 1572864 | tf_op jit(solution)/shard_map/jit(_flip)/rev | solution.py:190
  145.5 72.5 %while.66 = (s32[]{:T(128)}, f32[3,4,64,128]{3,2,1,0:T(8,128)S(1)}, f32[3,4]{1,0:T(4,128)S(1)}, f32[8,3,128,4,64]{2,4,3,1,0:T(8,128)}, f32[8,3,128,4]{3,2,1,0:T(...) while((s32[]{:T(128)}, f32[3,4,64,128]{3,2,1,0:T(8,128)S(1)}, ...), condition=%wide.region_9.10_spmd.clone, body=%wide.region_7.9_spmd.clone.sunk | while | flops 467358240 | bytes 3932897 | solution.py:91
  185.6 2.9 fusion.193
  194.7 2.9 fusion.193
  203.8 2.9 fusion.193
  212.8 2.9 fusion.193
  230.4 65.1 %while.64 = (s32[]{:T(128)}, f32[3,4,64,128]{3,2,1,0:T(8,128)S(1)}, f32[3,4]{1,0:T(4,128)S(1)}, f32[8,3,128,4,64]{2,4,3,1,0:T(8,128)}, f32[8,3,128,4]{3,2,1,0:T(...) while((s32[]{:T(128)}, f32[3,4,64,128]{3,2,1,0:T(8,128)S(1)}, ...), condition=%wide.region_4.5_spmd.clone, body=%wide.region_2.4_spmd.clone.sunk | while | flops 467358240 | bytes 3932897 | solution.py:91
  297.7 12.0 %all-gather.5 = f32[4,3,4]{2,1,0:T(4,128)S(1)} all-gather(f32[1,3,4]{2,1,0:T(4,128)S(1)} %bitcast.380), channel_id=4, replica_groups=mesh['groups'=2,'ctx'=4,'fsdp'=4] {'ctx'}, dimensions={0}, use_global_device_ids=true | all-gather | bytes 240 | tf_op jit(solution)/shard_map/all_gather | solution.py:22
  314.4 12.2 %all-gather.4 = f32[4,3,4]{2,1,0:T(4,128)S(1)} all-gather(f32[1,3,4]{2,1,0:T(4,128)S(1)} %bitcast.379), channel_id=2, replica_groups=mesh['groups'=2,'ctx'=4,'fsdp'=4] {'ctx'}, dimensions={0}, use_global_device_ids=true | all-gather | bytes 240 | tf_op jit(solution)/shard_map/all_gather | solution.py:22
  331.4 4.7 while.67
  336.1 5.0 bitcast_add_fusion.4
  341.2 6.7 %rev.23 = f32[3,1024,4,64]{1,3,2,0:T(8,128)} reverse(f32[3,1024,4,64]{1,3,2,0:T(8,128)} %bitcast_add_fusion.4), dimensions={1} | reverse | bytes 6291456 | tf_op jit(solution)/shard_map/jit(_flip)/rev | solution.py:204
  347.8 4.6 while.65
  352.4 6.9 %multiply_reduce_fusion = (f32[3,1024]{1,0:T(4,128)S(1)}, f32[3,1024,4,64]{1,3,2,0:T(8,128)}) fusion(bf16[3,1024,4,64]{1,3,2,0:T(8,128)(2,1)S(1)} %reshape.248, f32[4]{0:T(128)S(1)} %dynamic_slice.71, f32[3,1024,4,64]{1,3,2,0:T(8,128)} %rev.23, f32[3,4,64,128]{3,2,1,0:T(8,128)S(1)} %get-tuple-element.353, bf16[3,1024,4,128]{1,3,2,0:T(8,128)(2,1)} %bitcast.353, ...), kind=kOutput, calls=%fused_computation.119 | convolution fusion | flops 1214247936 | bytes 12251152 | tf_op jit(solution)/shard_map/vtn,vhpn->vthp/dot_general | solution.py:120
  361.7 10.4 %psum.7 = f32[3,1024]{1,0:T(4,128)S(1)} all-reduce(f32[3,1024]{1,0:T(4,128)S(1)} %get-tuple-element.690), channel_id=1, replica_groups=mesh['groups'=2,'ctx'=4,'fsdp'=4] {'fsdp'}, use_global_device_ids=true, to_apply=%region_13.14 | all-reduce | flops 3072 | bytes 24576 | tf_op jit(solution)/shard_map/psum | solution.py:208
  375.3 3.7 all-to-all-start.2
  379.4 25.3 %all-to-all-done.2 = bf16[3,1024,256]{2,0,1:T(4,128)(2,1)S(1)} async-done(((bf16[3,1024,256]{2,0,1:T(4,128)(2,1)}), bf16[3,1024,256]{2,0,1:T(4,128)(2,1)S(1)}, u32[]{:S(2)}, u32[]{:S(2)}) %all-to-all-start.2) | async-done | bytes 1572896 | tf_op jit(solution)/shard_map/all_to_all | solution.py:211
  407.7 4.3 add_convert_fusion
  416.0 5.6 %fusion.94 = f32[1024,1024]{1,0:T(8,128)} fusion(bf16[768,1024]{1,0:T(8,128)(2,1)} %bitcast.371, bf16[768,128]{1,0:T(8,128)(2,1)S(1)} %bitcast.373, bf16[1024,128]{1,0:T(8,128)(2,1)S(1)} %copy-done), kind=kOutput, calls=%fused_computation.127 | convolution fusion | flops 1812725760 | bytes 6225920 | tf_op jit(solution)/shard_map/dot_general | solution.py:238
  422.8 46.5 %reduce-scatter.5.cloned.1.call-done = f32[64,128]{1,0:T(8,128)} async-done(((f32[1024,128]{1,0:T(8,128)}), f32[64,128]{1,0:T(8,128)}) %reduce-scatter.5.cloned.1.call-update) | async-done | bytes 32784 | tf_op jit(solution)/shard_map/reduce_scatter | solution.py:245
  469.3 76.3 %reduce-scatter.3.cloned.1.call-done = f32[64,1024]{1,0:T(8,128)} async-done(((f32[1024,1024]{1,0:T(8,128)}), f32[64,1024]{1,0:T(8,128)}) %reduce-scatter.3.cloned.1.call-update) | async-done | bytes 262160 | tf_op jit(solution)/shard_map/reduce_scatter | solution.py:237
  (433 shorter events, 204.7 us)
Async XLA Ops:
  7.2 404.8 %copy-start = (bf16[1024,128]{1,0:T(8,128)(2,1)S(1)}, bf16[1024,128]{1,0:T(8,128)(2,1)}, u32[]{:S(2)}) copy-start(bf16[1024,128]{1,0:T(8,128)(2,1)} %param.33) | copy-start | bytes 786436
  7.2 4.0 copy-start.12
  7.2 33.7 %all-gather.12.cloned.1.call-start = ((), (), s32[]{:S(2)}) async-start(), calls=%async_computation.5 | async-start | bytes 3932160 | tf_op jit(solution)/shard_map/all_gather | solution.py:155
  7.9 102.7 %all-gather.14.cloned.1.call-start = ((), (), s32[]{:S(2)}) async-start(), calls=%async_computation.6 | async-start | bytes 3932160 | tf_op jit(solution)/shard_map/all_gather | solution.py:173
  11.7 33.9 %copy-start.8 = (bf16[3,256,1024]{2,1,0:T(8,128)(2,1)}, bf16[3,256,1024]{2,1,0:T(8,128)(2,1)S(1)}, u32[]{:S(2)}) copy-start(bf16[3,256,1024]{2,1,0:T(8,128)(2,1)S(1)} %multiply_convert_fusion.1) | copy-start | bytes 4718596
  45.5 1.4 copy-start.7
  47.0 1.3 copy-start.9
  47.0 6.5 %copy-start.13 = (f32[2,16]{1,0:T(2,128)S(1)}, f32[2,16]{1,0:T(2,128)}, u32[]{:S(2)}) copy-start(f32[2,16]{1,0:T(2,128)} %param.28) | copy-start | bytes 388
  54.9 8.9 %all-to-all-start = ((f32[3,256,2,4,4]{1,4,2,0,3:T(4,128)}), f32[3,256,2,4,4]{1,4,2,0,3:T(4,128)S(1)}, u32[]{:S(2)}, u32[]{:S(2)}) async-start(f32[3,256,2,4,4]{1,4,2,0,3:T(4,128)} %copy.246), calls=%async_computation | async-start | bytes 196608 | tf_op jit(solution)/shard_map/all_to_all | solution.py:171
  61.7 5.8 %copy-start.11 = (f32[2,16]{1,0:T(2,128)S(1)}, f32[2,16]{1,0:T(2,128)}, u32[]{:S(2)}) copy-start(f32[2,16]{1,0:T(2,128)} %param.29) | copy-start | bytes 388
  63.8 29.5 %all-to-all-start.1 = ((bf16[3,256,4,256]{1,3,0,2:T(8,128)(2,1)}), bf16[3,256,4,256]{1,3,0,2:T(8,128)(2,1)S(1)}, u32[]{:S(2)}, u32[]{:S(2)}) async-start(bf16[3,256,4,256]{1,3,0,2:T(8,128)(2,1)} %copy.249), calls=%async_computation.1 | async-start | bytes 3145728 | tf_op jit(solution)/shard_map/all_to_all | solution.py:168
  67.4 264.0 %all-gather.20.cloned.1.call-start = ((), (), s32[]{:S(2)}) async-start(), calls=%async_computation.11 | async-start | bytes 1966080 | tf_op jit(solution)/shard_map/all_gather | solution.py:22
  105.9 3.1 copy-start.5
  124.6 3.6 copy-start.3
  217.9 0.7 copy-start.2
  218.7 129.1 %all-gather.18.cloned.1.call-start = ((), (), s32[]{:S(2)}) async-start(), calls=%async_computation.10 | async-start | bytes 1966080 | tf_op jit(solution)/shard_map/all_gather | solution.py:22
  218.9 4.7 copy-start.6
  230.4 66.5 %copy-start.14 = (f32[16]{0:T(128)S(1)}, f32[16]{0:T(128)}, u32[]{:S(2)}) copy-start(f32[16]{0:T(128)} %param.30) | copy-start | bytes 196
  295.5 0.8 copy-start.1
  296.3 111.4 %all-gather.16.cloned.1.call-start = ((), (), s32[]{:S(2)}) async-start(), calls=%async_computation.7 | async-start | bytes 2621440 | tf_op jit(solution)/shard_map/all_gather | solution.py:216
  331.4 4.8 copy-start.4
  375.3 4.0 copy-start.10
  375.3 29.4 %all-to-all-start.2 = ((bf16[3,1024,256]{2,0,1:T(4,128)(2,1)}), bf16[3,1024,256]{2,0,1:T(4,128)(2,1)S(1)}, u32[]{:S(2)}, u32[]{:S(2)}) async-start(bf16[3,1024,256]{2,0,1:T(4,128)(2,1)} %copy.268), calls=%async_computation.2 | async-start | bytes 4194304 | tf_op jit(solution)/shard_map/all_to_all | solution.py:211
  379.0 90.3 %reduce-scatter.5.cloned.1.call-start = ((), (), s32[]{:S(2)}) async-start(), calls=%async_computation.9 | async-start | bytes 557056 | tf_op jit(solution)/shard_map/reduce_scatter | solution.py:245
  415.9 129.6 %reduce-scatter.3.cloned.1.call-start = ((), (), s32[]{:S(2)}) async-start(), calls=%async_computation.8 | async-start | bytes 4456448 | tf_op jit(solution)/shard_map/reduce_scatter | solution.py:237
Sparse Core Ops, SparseCore 0:
  9.6 31.2 all-gather.11
  48.4 35.9 all-gather.13
  218.8 37.0 all-gather.19
  296.4 37.3 all-gather.17
  335.2 21.4 all-gather.15
  416.1 53.1 reduce-scatter.4
  474.2 71.3 reduce-scatter.2
where the time goes:
time: 558 us; the launch traced here: 552 us
  waiting for transfers between devices  205 us (37%)
  matrix products  141 us (25%)
  local copies, waits for them, and re-layouts  107 us (19%)
  blocking collectives  39.8 us (7%)
  other arithmetic  32.1 us (6%)
  between operations  14.7 us (3%)
  starting transfers between devices  11.3 us (2%)
    reduce_scatter x1, waiting for transfers between devices, on_device(): lax.psum_scatter(lax.dot_general(columns, grad_hidden, (((0,), (0,)), (()...  76.3 us
    reduce_scatter x1, waiting for transfers between devices, on_device(): lax.psum_scatter(head_term, ('ctx', 'fsdp'), scatter_dimension=0, tiled=T...  46.5 us
    dot_general x16, matrix products, advance(): inside = jnp.einsum('tsh,shp->thp', mixing, value_float, precision=highest)  44.6 us
    all_gather x1, waiting for transfers between devices, on_device(): lax.all_gather(in_weight, 'fsdp', axis=0, tiled=True)  29.2 us
    dot_general x16, matrix products, advance(): jnp.einsum('tn,hpn->thp', read_float, state_now, precision=highest)  26 us
    all_to_all x1, waiting for transfers between devices, on_device(): lax.all_to_all(normed_heads, 'fsdp', split_axis=1, concat_axis=2, tiled=T...  25.3 us
    all_to_all x1, waiting for transfers between devices, on_device(): lax.all_to_all(value_rows, 'fsdp', split_axis=2, concat_axis=1, tiled=True)  24.8 us
    all_gather x2, blocking collectives, carried_in_2(): everything = jax.tree.map(lambda part: lax.all_gather(part, axis), value)  24.2 us
  transfers between devices with their start and end apart: 10, of which 6 were waited for; matrix products, arithmetic and copies ran while one was open for 28% of the time, Pallas kernels for 0%

commit v1 on v0

--- a/solution.py
+++ b/solution.py
@@ -15,6 +15,18 @@
 loss_scale = 256.0
 mix_lambda = 12.0
 highest = lax.Precision.HIGHEST
+
+
+def cut_along(x, dim, peers):
+    shape = x.shape
+    blocks = x.reshape(*shape[:dim], peers, shape[dim] // peers, *shape[dim + 1 :])
+    return jnp.moveaxis(blocks, dim, 0)
+
+
+def laid_out(blocks, dim):
+    shape = list(blocks.shape[1:])
+    shape[dim] *= blocks.shape[0]
+    return jnp.moveaxis(blocks, 0, dim).reshape(shape)
 
 
 def carried_in_2(value, axis, combine, identity, reverse):
@@ -208,7 +220,14 @@
     square_total = lax.psum(jnp.sum(mixed * mixed, axis=-1), "fsdp")
     scaling = lax.rsqrt(square_total / inner_width + 1e-05)
     normed_heads = (mixed * scaling[:, :, None] * local_gain[None, None, :]).astype(jnp.bfloat16)
-    normed_rows = lax.all_to_all(normed_heads, "fsdp", split_axis=1, concat_axis=2, tiled=True)
+    size, mine_2 = (lax.axis_size("fsdp"), lax.axis_index("fsdp"))
+    blocks = cut_along(normed_heads, 1, size)
+    outs = [blocks[mine_2]]
+    for hop in range(1, size):
+        sent = blocks[(mine_2 + hop) % size]
+        outs.append(lax.ppermute(sent, "fsdp", [(i, (i + hop) % size) for i in range(size)]))
+    blocks = jnp.stack(outs)[(mine_2 - jnp.arange(size)) % size]
+    normed_rows = laid_out(blocks, 2)
     normed = normed_rows.reshape(VIEWS * row_count, inner_width)
     columns = normed
     out_sum = jnp.dot(

time: 558 us -> 558 us (level)
  local copies, waits for them, and re-layouts: 107 us -> 118 us
  waiting for transfers between devices: 205 us -> 194 us
    all_to_all x1 -> x0, waiting for transfers between devices: 25.3 us -> none  [on_device(): lax.all_to_all(normed_heads, 'fsdp', split_axis=1, concat_axis=2, tiled=T...]
    ppermute x0 -> x3, waiting for transfers between devices: none -> 15.8 us  [on_device(): lax.ppermute(sent, 'fsdp', [(i, (i + hop) % size) for i in range(size)])]
    reshape x1 -> x2, local copies, waits for them, and re-layouts: 2.37 us -> 10 us  [on_device(): mixed = mixed.reshape(VIEWS, range_rows, local_heads * HEAD_DIM)]
    unnamed x39 -> x37, local copies, waits for them, and re-layouts: 16 us -> 17 us
  transfers between devices with their start and end apart: 10 -> 12, of which waited for: 6 -> 7; matrix products, arithmetic and copies ran while one was open for 28% -> 31% of each run, Pallas kernels for 0% -> 0%
where the time goes in v1:
time: 558 us; the launch traced here: 553 us
  waiting for transfers between devices  194 us (35%)
  matrix products  141 us (25%)
  local copies, waits for them, and re-layouts  118 us (21%)
  blocking collectives  39.6 us (7%)
  other arithmetic  35.4 us (6%)
  between operations  14.7 us (3%)
  starting transfers between devices  9.4 us (2%)
    reduce_scatter x1, waiting for transfers between devices, on_device(): lax.psum_scatter(lax.dot_general(columns, grad_hidden, (((0,), (0,)), (()...  76.3 us
    reduce_scatter x1, waiting for transfers between devices, on_device(): lax.psum_scatter(head_term, ('ctx', 'fsdp'), scatter_dimension=0, tiled=T...  48.3 us
    dot_general x16, matrix products, advance(): inside = jnp.einsum('tsh,shp->thp', mixing, value_float, precision=highest)  44.6 us
    all_gather x1, waiting for transfers between devices, on_device(): lax.all_gather(in_weight, 'fsdp', axis=0, tiled=True)  28 us
    dot_general x16, matrix products, advance(): jnp.einsum('tn,hpn->thp', read_float, state_now, precision=highest)  26 us
    all_to_all x1, waiting for transfers between devices, on_device(): lax.all_to_all(value_rows, 'fsdp', split_axis=2, concat_axis=1, tiled=True)  24.5 us
    all_gather x2, blocking collectives, carried_in_2(): everything = jax.tree.map(lambda part: lax.all_gather(part, axis), value)  24.1 us
    dot_general x16, matrix products, advance(): jnp.einsum('shp,sn->hpn', weighted, write_float, precision=highest)  22.5 us
  transfers between devices with their start and end apart: 12, of which 7 were waited for; matrix products, arithmetic and copies ran while one was open for 31% of the time, Pallas kernels for 0%

profile of v1, /device:TPU:0, one launch (start us, length us, event | category | flops | bytes accessed | tf_op | source)
XLA Modules:
  0.0 553.1 jit_solution(4162645939532604132)
XLA Ops:
  12.9 28.0 %all-gather.12.cloned.1.call-done = bf16[1024,1536]{1,0:T(8,128)(2,1)} async-done(((bf16[256,1536]{1,0:T(8,128)(2,1)}), bf16[1024,1536]{1,0:T(8,128)(2,1)}) %all-gather.12.cloned.1.call-update) | async-done | bytes 3145744 | tf_op jit(solution)/shard_map/all_gather | solution.py:167
  40.8 5.0 convolution_convert_fusion
  48.6 5.2 all_gather.36
  55.1 3.3 all-to-all-start
  64.3 3.7 all-to-all-start.1
  69.1 24.5 %all-to-all-done.1 = bf16[3,256,4,256]{1,3,0,2:T(8,128)(2,1)S(1)} async-done(((bf16[3,256,4,256]{1,3,0,2:T(8,128)(2,1)}), bf16[3,256,4,256]{1,3,0,2:T(8,128)(2,1)S(1)}, u32[]{:S(2)}, u32[]{:S(2)}) %all-to-all-start.1) | async-done | bytes 1572896 | tf_op jit(solution)/shard_map/all_to_all | solution.py:180
  98.9 3.6 reshape_reshape.6
  102.5 3.7 rev.20
  106.2 3.1 copy.148
  110.9 3.6 fusion.118
  114.6 10.3 %rev.22 = bf16[3,1024,128]{1,2,0:T(8,128)(2,1)S(1)} reverse(bf16[3,1024,128]{1,2,0:T(8,128)(2,1)} %get-tuple-element.620), dimensions={1} | reverse | bytes 1572864 | tf_op jit(solution)/shard_map/jit(_flip)/rev | solution.py:199
  128.5 10.3 %rev.21 = bf16[3,1024,128]{1,2,0:T(8,128)(2,1)S(1)} reverse(bf16[3,1024,128]{1,2,0:T(8,128)(2,1)} %get-tuple-element.621), dimensions={1} | reverse | bytes 1572864 | tf_op jit(solution)/shard_map/jit(_flip)/rev | solution.py:202
  145.8 72.5 %while.66 = (s32[]{:T(128)}, f32[3,4,64,128]{3,2,1,0:T(8,128)S(1)}, f32[3,4]{1,0:T(4,128)S(1)}, f32[8,3,128,4,64]{2,4,3,1,0:T(8,128)}, f32[8,3,128,4]{3,2,1,0:T(...) while((s32[]{:T(128)}, f32[3,4,64,128]{3,2,1,0:T(8,128)S(1)}, ...), condition=%wide.region_9.10_spmd.clone, body=%wide.region_7.9_spmd.clone.sunk | while | flops 467358240 | bytes 3932897 | solution.py:103
  195.0 2.9 fusion.195
  204.1 2.9 fusion.195
  230.7 65.2 %while.64 = (s32[]{:T(128)}, f32[3,4,64,128]{3,2,1,0:T(8,128)S(1)}, f32[3,4]{1,0:T(4,128)S(1)}, f32[8,3,128,4,64]{2,4,3,1,0:T(8,128)}, f32[8,3,128,4]{3,2,1,0:T(...) while((s32[]{:T(128)}, f32[3,4,64,128]{3,2,1,0:T(8,128)S(1)}, ...), condition=%wide.region_4.5_spmd.clone, body=%wide.region_2.4_spmd.clone.sunk | while | flops 467358240 | bytes 3932897 | solution.py:103
  298.2 12.0 %all-gather.5 = f32[4,3,4]{2,1,0:T(4,128)S(1)} all-gather(f32[1,3,4]{2,1,0:T(4,128)S(1)} %bitcast.397), channel_id=4, replica_groups=mesh['groups'=2,'ctx'=4,'fsdp'=4] {'ctx'}, dimensions={0}, use_global_device_ids=true | all-gather | bytes 240 | tf_op jit(solution)/shard_map/all_gather | solution.py:34
  315.0 12.1 %all-gather.4 = f32[4,3,4]{2,1,0:T(4,128)S(1)} all-gather(f32[1,3,4]{2,1,0:T(4,128)S(1)} %bitcast.396), channel_id=2, replica_groups=mesh['groups'=2,'ctx'=4,'fsdp'=4] {'ctx'}, dimensions={0}, use_global_device_ids=true | all-gather | bytes 240 | tf_op jit(solution)/shard_map/all_gather | solution.py:34
  331.8 4.7 while.67
  336.5 5.0 bitcast_add_fusion.4
  341.6 6.7 %rev.23 = f32[3,1024,4,64]{1,3,2,0:T(8,128)} reverse(f32[3,1024,4,64]{1,3,2,0:T(8,128)} %bitcast_add_fusion.4), dimensions={1} | reverse | bytes 6291456 | tf_op jit(solution)/shard_map/jit(_flip)/rev | solution.py:216
  348.3 4.6 while.65
  352.9 6.9 %multiply_reduce_fusion = (f32[3,1024]{1,0:T(4,128)S(1)}, f32[3,1024,4,64]{1,3,2,0:T(8,128)}) fusion(bf16[3,1024,4,64]{1,3,2,0:T(8,128)(2,1)S(1)} %reshape.304, f32[4]{0:T(128)S(1)} %dynamic_slice.77, f32[3,1024,4,64]{1,3,2,0:T(8,128)} %rev.23, f32[3,4,64,128]{3,2,1,0:T(8,128)S(1)} %get-tuple-element.353, bf16[3,1024,4,128]{1,3,2,0:T(8,128)(2,1)} %bitcast.367, ...), kind=kOutput, calls=%fused_computation.120 | convolution fusion | flops 1214247936 | bytes 12251152 | tf_op jit(solution)/shard_map/vtn,vhpn->vthp/dot_general | solution.py:132
  359.9 5.2 reshape.309
  365.0 4.9 copy.159
  369.9 10.2 %psum.7 = f32[3,1024]{1,0:T(4,128)S(1)} all-reduce(f32[3,1024]{1,0:T(4,128)S(1)} %get-tuple-element.634), channel_id=1, replica_groups=mesh['groups'=2,'ctx'=4,'fsdp'=4] {'fsdp'}, use_global_device_ids=true, to_apply=%region_13.14 | all-reduce | flops 3072 | bytes 24576 | tf_op jit(solution)/shard_map/psum | solution.py:220
  384.7 8.8 %collective-permute-done = bf16[3,256,256]{2,1,0:T(8,128)(2,1)S(1)} collective-permute-done((bf16[3,256,256]{2,1,0:T(8,128)(2,1)S(1)}, bf16[3,256,256]{2,1,0:T(8,128)(2,1)S(1)}, u32[]{:S(2)}, u32[]{:S(2)}) %collective-permute-start) | collective-permute-done | bytes 393248 | tf_op jit(solution)/shard_map/ppermute | solution.py:228
  394.7 5.8 %collective-permute-done.2 = bf16[3,256,256]{2,1,0:T(8,128)(2,1)S(1)} collective-permute-done((bf16[3,256,256]{2,1,0:T(8,128)(2,1)S(1)}, bf16[3,256,256]{2,1,0:T(8,128)(2,1)S(1)}, u32[]{:S(2)}, u32[]{:S(2)}) %collective-permute-start.2) | collective-permute-done | bytes 393248 | tf_op jit(solution)/shard_map/ppermute | solution.py:228
  406.7 4.3 add_convert_fusion
  414.9 5.6 %fusion.94 = f32[1024,1024]{1,0:T(8,128)} fusion(bf16[768,1024]{1,0:T(8,128)(2,1)} %bitcast.385, bf16[768,128]{1,0:T(8,128)(2,1)S(1)} %bitcast.387, bf16[1024,128]{1,0:T(8,128)(2,1)S(1)} %copy-done), kind=kOutput, calls=%fused_computation.129 | convolution fusion | flops 1812725760 | bytes 6225920 | tf_op jit(solution)/shard_map/dot_general | solution.py:257
  421.7 48.3 %reduce-scatter.5.cloned.1.call-done = f32[64,128]{1,0:T(8,128)} async-done(((f32[1024,128]{1,0:T(8,128)}), f32[64,128]{1,0:T(8,128)}) %reduce-scatter.5.cloned.1.call-update) | async-done | bytes 32784 | tf_op jit(solution)/shard_map/reduce_scatter | solution.py:264
  470.0 76.3 %reduce-scatter.3.cloned.1.call-done = f32[64,1024]{1,0:T(8,128)} async-done(((f32[1024,1024]{1,0:T(8,128)}), f32[64,1024]{1,0:T(8,128)}) %reduce-scatter.3.cloned.1.call-update) | async-done | bytes 262160 | tf_op jit(solution)/shard_map/reduce_scatter | solution.py:256
  (439 shorter events, 215.1 us)
Async XLA Ops:
  7.2 403.8 %copy-start = (bf16[1024,128]{1,0:T(8,128)(2,1)S(1)}, bf16[1024,128]{1,0:T(8,128)(2,1)}, u32[]{:S(2)}) copy-start(bf16[1024,128]{1,0:T(8,128)(2,1)} %param.33) | copy-start | bytes 786436
  7.2 4.0 copy-start.11
  7.2 33.7 %all-gather.12.cloned.1.call-start = ((), (), s32[]{:S(2)}) async-start(), calls=%async_computation.4 | async-start | bytes 3932160 | tf_op jit(solution)/shard_map/all_gather | solution.py:167
  7.9 103.0 %all-gather.14.cloned.1.call-start = ((), (), s32[]{:S(2)}) async-start(), calls=%async_computation.5 | async-start | bytes 3932160 | tf_op jit(solution)/shard_map/all_gather | solution.py:185
  45.8 1.4 copy-start.7
  47.3 1.3 copy-start.8
  47.3 6.5 %copy-start.12 = (f32[2,16]{1,0:T(2,128)S(1)}, f32[2,16]{1,0:T(2,128)}, u32[]{:S(2)}) copy-start(f32[2,16]{1,0:T(2,128)} %param.28) | copy-start | bytes 388
  55.1 9.1 %all-to-all-start = ((f32[3,256,2,4,4]{1,4,2,0,3:T(4,128)}), f32[3,256,2,4,4]{1,4,2,0,3:T(4,128)S(1)}, u32[]{:S(2)}, u32[]{:S(2)}) async-start(f32[3,256,2,4,4]{1,4,2,0,3:T(4,128)} %copy.138), calls=%async_computation | async-start | bytes 196608 | tf_op jit(solution)/shard_map/all_to_all | solution.py:183
  64.3 3.8 copy-start.10
  64.3 29.3 %all-to-all-start.1 = ((bf16[3,256,4,256]{1,3,0,2:T(8,128)(2,1)}), bf16[3,256,4,256]{1,3,0,2:T(8,128)(2,1)S(1)}, u32[]{:S(2)}, u32[]{:S(2)}) async-start(bf16[3,256,4,256]{1,3,0,2:T(8,128)(2,1)} %copy.141), calls=%async_computation.1 | async-start | bytes 3145728 | tf_op jit(solution)/shard_map/all_to_all | solution.py:180
  68.0 263.8 %all-gather.20.cloned.1.call-start = ((), (), s32[]{:S(2)}) async-start(), calls=%async_computation.10 | async-start | bytes 1966080 | tf_op jit(solution)/shard_map/all_gather | solution.py:34
  106.2 3.1 copy-start.5
  124.9 3.6 copy-start.3
  218.2 0.7 copy-start.2
  219.0 129.3 %all-gather.18.cloned.1.call-start = ((), (), s32[]{:S(2)}) async-start(), calls=%async_computation.9 | async-start | bytes 1966080 | tf_op jit(solution)/shard_map/all_gather | solution.py:34
  219.2 4.7 copy-start.6
  230.7 66.7 %copy-start.13 = (f32[16]{0:T(128)S(1)}, f32[16]{0:T(128)}, u32[]{:S(2)}) copy-start(f32[16]{0:T(128)} %param.30) | copy-start | bytes 196
  295.8 0.8 copy-start.1
  296.7 110.0 %all-gather.16.cloned.1.call-start = ((), (), s32[]{:S(2)}) async-start(), calls=%async_computation.6 | async-start | bytes 2621440 | tf_op jit(solution)/shard_map/all_gather | solution.py:235
  297.2 172.8 %reduce-scatter.5.cloned.1.call-start = ((), (), s32[]{:S(2)}) async-start(), calls=%async_computation.8 | async-start | bytes 557056 | tf_op jit(solution)/shard_map/reduce_scatter | solution.py:264
  331.8 4.8 copy-start.4
  382.5 2.1 copy-start.9
  382.6 10.9 %collective-permute-start = (bf16[3,256,256]{2,1,0:T(8,128)(2,1)S(1)}, bf16[3,256,256]{2,1,0:T(8,128)(2,1)S(1)}, u32[]{:S(2)}, u32[]{:S(2)}) collective-permute-start(bf16[3,256,256]{2,1,0:T(8,128)(2,1)S(1)} %get-tuple-element.626), channel_id=1, source_target_pairs={{0,1},{1,2},{2,3},{3,0},{4,5},{5,6},{6,7},{7,4},{8,9},{9,10},{10,1... | collective-permute-start | bytes 1179656 | tf_op jit(solution)/shard_map/ppermute | solution.py:228
  382.7 12.0 %collective-permute-start.1 = (bf16[3,256,256]{2,1,0:T(8,128)(2,1)S(1)}, bf16[3,256,256]{2,1,0:T(8,128)(2,1)S(1)}, u32[]{:S(2)}, u32[]{:S(2)}) collective-permute-start(bf16[3,256,256]{2,1,0:T(8,128)(2,1)S(1)} %get-tuple-element.625), channel_id=1, source_target_pairs={{0,2},{1,3},{2,0},{3,1},{4,6},{5,7},{6,4},{7,5},{8,10},{9,11},{10,... | collective-permute-start | bytes 1179656 | tf_op jit(solution)/shard_map/ppermute | solution.py:228
  383.2 17.3 %collective-permute-start.2 = (bf16[3,256,256]{2,1,0:T(8,128)(2,1)S(1)}, bf16[3,256,256]{2,1,0:T(8,128)(2,1)S(1)}, u32[]{:S(2)}, u32[]{:S(2)}) collective-permute-start(bf16[3,256,256]{2,1,0:T(8,128)(2,1)S(1)} %get-tuple-element.624), channel_id=1, source_target_pairs={{0,3},{1,0},{2,1},{3,2},{4,7},{5,4},{6,5},{7,6},{8,11},{9,8},{10,9... | collective-permute-start | bytes 1179656 | tf_op jit(solution)/shard_map/ppermute | solution.py:228
  414.9 131.4 %reduce-scatter.3.cloned.1.call-start = ((), (), s32[]{:S(2)}) async-start(), calls=%async_computation.7 | async-start | bytes 4456448 | tf_op jit(solution)/shard_map/reduce_scatter | solution.py:256
Sparse Core Ops, SparseCore 0:
  9.6 31.2 all-gather.11
  48.7 35.6 all-gather.13
  219.1 37.0 all-gather.19
  296.8 37.2 all-gather.17
  335.5 21.4 all-gather.15
  415.0 54.9 reduce-scatter.4
  474.9 71.3 reduce-scatter.2
